TPU v7x, 32 devices: a whole 2x2x4 slice. The times are simulated.
32 devices in a mesh: ens: 4 (over z), gx: 2 (over x), gy: 4 (over y, core).
Axes of the slice: x: 2, y: 2, z: 4, core: 2. Of those that a mesh axis runs over, the one named last changes fastest.
Arguments:
- members: bfloat16 [64, 75, 32, 512], P(('ens', 'gx'), None, None, 'gy'), may hold values from -0.75 to 0.75
- spread: bfloat16 [75, 75], replicated, as said below
- sea_mask: int32 [32, 512], P(('ens', 'gx'), 'gy'), may hold values 0 or 1
- innovations: float32 [75, 32, 512], P(None, ('ens', 'gx'), 'gy'), may hold values from -19 to 19
- obs_error: float32 [75, 32, 512], P(None, ('ens', 'gx'), 'gy'), may hold values from 0.3 to 3
- static_scale: float32 [75, 32, 512], P(None, ('ens', 'gx'), 'gy'), may hold values from 2 to 8
Outputs:
- increment: float32 [75, 32, 512], P(None, ('ens', 'gx'), 'gy')
- alpha_fields: bfloat16 [64, 75, 32, 512], P(('ens', 'gx'), None, None, 'gy')
Inputs may be any that keep to these rules, and one draw needn't show every extreme that they name: `spread`: symmetric and positive definite. `sea_mask`: 1 marks sea, 0 land.
All inputs are finite; a program needn't handle non-finite values. No bound on the sum of `sea_mask` on one device may be relied on, other than what follows from the above.
Results may differ from a plain program's by a relative error of at most 0.0065.
Values may be sent and summed in bfloat16 or wider, within the bound.
A program may use at most 128 MiB of HBM per device.

v0:
```python
import jax
import jax.numpy as jnp
from jax import lax
from jax.sharding import PartitionSpec as P

GRIDS = 3
SWEEPS = 2
COARSE_SWEEPS = 4
ITERATIONS = 3


diffusivity = 16.0
damping = 0.8


def with_halo(x, sides, width):
    for axis, dim in sides:
        size, length = (lax.axis_size(axis), x.shape[dim])
        up = [(i, (i + 1) % size) for i in range(size - 1)]
        down = [(j, i) for i, j in up]
        last = lax.slice_in_dim(x, length - width, length, axis=dim)
        leading = lax.slice_in_dim(x, 0, width, axis=dim)
        before = lax.ppermute(last, axis, up)
        after = lax.ppermute(leading, axis, down)
        x = jnp.concatenate([before, x, after], axis=dim)
    return x


def neighbours(padded):
    return padded[:, 2:, 1:-1] + padded[:, :-2, 1:-1] + padded[:, 1:-1, 2:] + padded[:, 1:-1, :-2]


def apply_level(values, strength, padded):
    return values + strength * (4.0 * values - neighbours(padded))


def relax(values, source, strength, padded):
    return values + damping * (source - apply_level(values, strength, padded)) / (
        1.0 + 4.0 * strength
    )


def framed(values):
    return with_halo(values.astype(jnp.bfloat16), ((("ens", "gx"), 1), ("gy", 2)), 1).astype(
        values.dtype
    )


def restrict(values):
    layer_count, row_count, column_count = values.shape
    return 0.25 * values.reshape(layer_count, row_count // 2, 2, column_count // 2, 2).sum(
        axis=(2, 4)
    )


def prolong(values):
    layer_count, row_count, column_count = values.shape
    spread_out = jnp.broadcast_to(
        values[:, :, None, :, None], (layer_count, row_count, 2, column_count, 2)
    )
    return spread_out.reshape(layer_count, 2 * row_count, 2 * column_count)


def coarse_solve(source, strength):
    factor = damping / (1.0 + 4.0 * strength)
    solution = factor * source
    for sweep_index in range(COARSE_SWEEPS - 1):
        padded = with_halo(solution, ((("ens", "gx"), 1), ("gy", 2)), 1)
        solution = relax(solution, source, strength, padded)
    return solution


def vcycle(source, grid_level):
    strength = diffusivity / 4.0**grid_level
    if grid_level == GRIDS - 1:
        return coarse_solve(source, strength)
    solution = damping / (1.0 + 4.0 * strength) * source
    solution = relax(solution, source, strength, framed(solution))
    remainder = source - apply_level(solution, strength, framed(solution))
    solution = solution + prolong(vcycle(restrict(remainder), grid_level + 1))
    for sweep_index in range(SWEEPS):
        solution = relax(solution, source, strength, framed(solution))
    return solution


def member_products(tiles, spread, masked):
    member_count, layer_count, row_count, column_count = tiles.shape
    product = (tiles * masked).astype(jnp.bfloat16)
    flat = product.reshape(member_count, layer_count, row_count * column_count)
    mixed = jnp.einsum("ij,kjc->kic", spread, flat, preferred_element_type=jnp.float32)
    return mixed.reshape(tiles.shape)


def local(members, spread, sea_mask, innovations, obs_error, static_scale):
    tiles = lax.all_to_all(members, ("ens", "gx"), split_axis=2, concat_axis=0, tiled=True)
    sea = sea_mask.astype(jnp.float32)[None]

    def covariance(direction):
        masked = sea * direction
        mixed = member_products(tiles, spread, masked)
        ensemble = jnp.sum(tiles * mixed, axis=0)
        static = static_scale * vcycle(static_scale * masked, 0)
        return sea * (ensemble + static)

    def system(direction):
        cov_dir = covariance(direction)
        return (cov_dir, cov_dir + obs_error * direction)

    def merged(residual, image):
        return lax.psum(
            (jnp.sum(residual * residual), jnp.sum(residual * image)), ("ens", "gx", "gy")
        )

    weights = jnp.zeros_like(innovations)
    increment = jnp.zeros_like(innovations)
    residual = innovations
    cov_res, image_res = system(residual)
    norm_now, product = merged(residual, image_res)
    alpha = norm_now / product
    direction, along, cov_dir = (residual, image_res, cov_res)
    for iteration in range(ITERATIONS):
        weights = weights + alpha * direction
        increment = increment + alpha * cov_dir
        residual = residual - alpha * along
        if iteration + 1 < ITERATIONS:
            cov_res, image_res = system(residual)
            norm_next, product = merged(residual, image_res)
            ratio = norm_next / norm_now
            alpha = norm_next / (product - ratio * norm_next / alpha)
            direction = residual + ratio * direction
            along = image_res + ratio * along
            cov_dir = cov_res + ratio * cov_dir
            norm_now = norm_next
    final = member_products(tiles, spread, sea * weights).astype(jnp.bfloat16)
    alpha_fields = lax.all_to_all(final, ("ens", "gx"), split_axis=0, concat_axis=2, tiled=True)
    return (increment, alpha_fields)


def solution(mesh):
    in_specs = (
        P(("ens", "gx"), None, None, "gy"),
        P(),
        P(("ens", "gx"), "gy"),
        P(None, ("ens", "gx"), "gy"),
        P(None, ("ens", "gx"), "gy"),
        P(None, ("ens", "gx"), "gy"),
    )
    out_specs = (P(None, ("ens", "gx"), "gy"), P(("ens", "gx"), None, None, "gy"))
    return jax.shard_map(local, mesh=mesh, in_specs=in_specs, out_specs=out_specs, check_vma=False)
```

profile of v0, /device:TPU:0, one launch (start us, length us, event | category | flops | bytes accessed | tf_op | source)
XLA Modules:
  0.0 999.4 jit_solution(5653683914160906844)
XLA Ops:
  0.6 6.5 copy.75
  7.2 7.4 all-to-all-start
  21.0 12.7 %collective-permute-done.1 = bf16[75,1,128]{0,2,1:T(8,128)(2,1)S(1)} collective-permute-done((bf16[75,1,128]{0,2,1:T(8,128)(2,1)S(1)}, bf16[75,1,128]{0,2,1:T(8,128)(2,1)S(1)}, u32[]{:S(2)}, u32[]{:S(2)}) %collective-permute-start.1) | collective-permute-done | bytes 19232 | tf_op jit(solution)/shard_map/ppermute | solution.py:24
  33.6 21.9 %collective-permute-done = bf16[75,1,128]{0,2,1:T(8,128)(2,1)S(1)} collective-permute-done((bf16[75,1,128]{0,2,1:T(8,128)(2,1)S(1)}, bf16[75,1,128]{0,2,1:T(8,128)(2,1)S(1)}, u32[]{:S(2)}, u32[]{:S(2)}) %collective-permute-start) | collective-permute-done | bytes 19232 | tf_op jit(solution)/shard_map/ppermute | solution.py:23
  62.2 43.9 %collective-permute-start.4 = (bf16[75,1,128]{0,2,1:T(8,128)(2,1)S(1)}, bf16[75,1,128]{0,2,1:T(8,128)(2,1)S(1)}, u32[]{:S(2)}, u32[]{:S(2)}) collective-permute-start(bf16[75,1,128]{0,2,1:T(8,128)(2,1)S(1)} %get-tuple-element.108), channel_id=1, source_target_pairs={{0,4},{4,8},{8,12},{12,16},{16,20},{20,24},{24,28},{1,5},{5,9},{9,... | collective-permute-start | bytes 57608 | tf_op jit(solution)/shard_map/ppermute | solution.py:23
  115.6 19.2 %collective-permute-start.8 = (bf16[75,1,64]{0,2,1:T(8,128)(2,1)S(1)}, bf16[75,1,64]{0,2,1:T(8,128)(2,1)S(1)}, u32[]{:S(2)}, u32[]{:S(2)}) collective-permute-start(bf16[75,1,64]{0,2,1:T(8,128)(2,1)S(1)} %get-tuple-element.176), channel_id=1, source_target_pairs={{0,4},{4,8},{8,12},{12,16},{16,20},{20,24},{24,28},{1,5},{5,9},{9,... | collective-permute-start | bytes 28808 | tf_op jit(solution)/shard_map/ppermute | solution.py:23
  142.8 16.9 %collective-permute-start.12 = (bf16[75,1,64]{0,2,1:T(8,128)(2,1)S(1)}, bf16[75,1,64]{0,2,1:T(8,128)(2,1)S(1)}, u32[]{:S(2)}, u32[]{:S(2)}) collective-permute-start(bf16[75,1,64]{0,2,1:T(8,128)(2,1)S(1)} %get-tuple-element.174), channel_id=1, source_target_pairs={{0,4},{4,8},{8,12},{12,16},{16,20},{20,24},{24,28},{1,5},{5,9},{9,... | collective-permute-start | bytes 28808 | tf_op jit(solution)/shard_map/ppermute | solution.py:23
  218.4 5.7 collective-permute-start.28
  233.1 5.7 collective-permute-start.32
  263.4 5.7 collective-permute-start.40
  278.8 9.2 copy.134
  288.0 12.5 %reshape.178 = f32[64,75,512]{2,0,1:T(8,128)} reshape(f32[8,8,75,4,128]{4,3,1,0,2:T(4,128)} %bitcast.87) | data formatting | bytes 19660800 | tf_op jit(solution)/shard_map/convert_element_type | solution.py:101
  300.5 5.7 multiply_convert_fusion.3
  307.1 9.6 fusion.2
  319.6 49.7 %all-reduce.2 = (f32[]{:T(128)}, f32[]{:T(128)}) all-reduce(f32[]{:T(128)} %multiply_reduce_fusion.5, f32[]{:T(128)} %get-tuple-element.47), channel_id=1, replica_groups=mesh['ens'=4,'gx'=2,'gy'=4] {'ens','gx','gy'}, use_global_device_ids=true, to_apply=%region_1.0 | all-reduce | flops 2 | bytes 16 | tf_op jit(solution)/shard_map/psum | solution.py:110
  393.5 15.3 %collective-permute-start.50 = (bf16[75,6,1]{0,2,1:T(2,128)(2,1)S(1)}, bf16[75,6,1]{0,2,1:T(2,128)(2,1)S(1)}, u32[]{:S(2)}, u32[]{:S(2)}) collective-permute-start(bf16[75,6,1]{0,2,1:T(2,128)(2,1)S(1)} %get-tuple-element.76), channel_id=1, source_target_pairs={{0,1},{1,2},{2,3},{4,5},{5,6},{6,7},{8,9},{9,10},{10,11},{12,13},{... | collective-permute-start | bytes 2708 | tf_op jit(solution)/shard_map/ppermute | solution.py:23
  410.6 5.7 collective-permute-start.52
  425.7 5.7 collective-permute-start.56
  533.5 6.0 collective-permute-start.84
  539.5 7.8 multiply_convert_fusion.2
  554.0 11.1 %fusion.1 = f32[75,512]{1,0:T(8,128)S(1)} fusion(f32[64,75,512]{2,0,1:T(8,128)S(1)} %bitcast.84, bf16[64,75,512]{2,0,1:T(8,128)(2,1)} %multiply_convert_fusion.2, bf16[75,75]{1,0:T(8,128)(2,1)S(1)} %copy-done), kind=kOutput, calls=%fused_computation.3 | convolution fusion | flops 373516800 | bytes 14910450 | tf_op jit(solution)/shard_map/ij,kjc->kic/dot_general | solution.py:90
  567.2 45.7 %all-reduce.1 = (f32[]{:T(128)}, f32[]{:T(128)}) all-reduce(f32[]{:T(128)} %get-tuple-element.9, f32[]{:T(128)} %get-tuple-element.8), channel_id=1, replica_groups=mesh['ens'=4,'gx'=2,'gy'=4] {'ens','gx','gy'}, use_global_device_ids=true, to_apply=%region_9.0 | all-reduce | flops 2 | bytes 16 | tf_op jit(solution)/shard_map/psum | solution.py:110
  646.8 5.7 collective-permute-start.96
  661.7 5.7 collective-permute-start.100
  773.9 6.0 collective-permute-start.128
  779.9 7.8 multiply_convert_fusion.1
  794.5 11.8 %fusion = f32[75,512]{1,0:T(8,128)} fusion(f32[64,75,512]{2,0,1:T(8,128)S(1)} %bitcast.86, bf16[64,75,512]{2,0,1:T(8,128)(2,1)} %multiply_convert_fusion.1, bf16[75,75]{1,0:T(8,128)(2,1)S(1)} %copy-done), kind=kOutput, calls=%fused_computation.1 | convolution fusion | flops 373516800 | bytes 14910450 | tf_op jit(solution)/shard_map/ij,kjc->kic/dot_general | solution.py:90
  809.2 44.9 %all-reduce = (f32[]{:T(128)}, f32[]{:T(128)}) all-reduce(f32[]{:T(128)} %get-tuple-element.11, f32[]{:T(128)} %get-tuple-element.10), channel_id=1, replica_groups=mesh['ens'=4,'gx'=2,'gy'=4] {'ens','gx','gy'}, use_global_device_ids=true, to_apply=%region_17.0 | all-reduce | flops 2 | bytes 16 | tf_op jit(solution)/shard_map/psum | solution.py:110
  864.3 6.3 convert_bitcast_fusion
  870.6 9.3 reshape.181
  886.0 107.0 %all-to-all-done.1 = bf16[64,75,4,128]{3,2,1,0:T(4,128)(2,1)} async-done(((bf16[64,75,4,128]{3,2,1,0:T(4,128)(2,1)}), bf16[64,75,4,128]{3,2,1,0:T(4,128)(2,1)}, u32[]{:S(2)}, u32[]{:S(2)}) %all-to-all-start.1) | async-done | bytes 4915232 | tf_op jit(solution)/shard_map/all_to_all | solution.py:135
  992.9 6.3 copy.108
  (433 shorter events, 445.4 us)
Async XLA Ops:
  7.2 271.6 %all-to-all-start = ((bf16[8,75,32,128]{3,0,1,2:T(8,128)(2,1)}), bf16[8,75,32,128]{3,0,1,2:T(8,128)(2,1)}, u32[]{:S(2)}, u32[]{:S(2)}) async-start(bf16[8,75,32,128]{3,0,1,2:T(8,128)(2,1)} %copy.75), calls=%async_computation | async-start | bytes 9830400 | tf_op jit(solution)/shard_map/all_to_all | solution.py:95
  15.1 18.5 %collective-permute-start.1 = (bf16[75,1,128]{0,2,1:T(8,128)(2,1)S(1)}, bf16[75,1,128]{0,2,1:T(8,128)(2,1)S(1)}, u32[]{:S(2)}, u32[]{:S(2)}) collective-permute-start(bf16[75,1,128]{0,2,1:T(8,128)(2,1)S(1)} %get-tuple-element.111), channel_id=1, source_target_pairs={{4,0},{8,4},{12,8},{16,12},{20,16},{24,20},{28,24},{5,1},{9,5},{13... | collective-permute-start | bytes 57608 | tf_op jit(solution)/shard_map/ppermute | solution.py:24
  16.4 39.1 %collective-permute-start = (bf16[75,1,128]{0,2,1:T(8,128)(2,1)S(1)}, bf16[75,1,128]{0,2,1:T(8,128)(2,1)S(1)}, u32[]{:S(2)}, u32[]{:S(2)}) collective-permute-start(bf16[75,1,128]{0,2,1:T(8,128)(2,1)S(1)} %get-tuple-element.110), channel_id=1, source_target_pairs={{0,4},{4,8},{8,12},{12,16},{16,20},{20,24},{24,28},{1,5},{5,9},{9,... | collective-permute-start | bytes 57608 | tf_op jit(solution)/shard_map/ppermute | solution.py:23
  60.9 45.2 %collective-permute-start.5 = (bf16[75,1,128]{0,2,1:T(8,128)(2,1)S(1)}, bf16[75,1,128]{0,2,1:T(8,128)(2,1)S(1)}, u32[]{:S(2)}, u32[]{:S(2)}) collective-permute-start(bf16[75,1,128]{0,2,1:T(8,128)(2,1)S(1)} %get-tuple-element.109), channel_id=1, source_target_pairs={{4,0},{8,4},{12,8},{16,12},{20,16},{24,20},{28,24},{5,1},{9,5},{13... | collective-permute-start | bytes 57608 | tf_op jit(solution)/shard_map/ppermute | solution.py:24
  62.2 46.5 %collective-permute-start.4 = (bf16[75,1,128]{0,2,1:T(8,128)(2,1)S(1)}, bf16[75,1,128]{0,2,1:T(8,128)(2,1)S(1)}, u32[]{:S(2)}, u32[]{:S(2)}) collective-permute-start(bf16[75,1,128]{0,2,1:T(8,128)(2,1)S(1)} %get-tuple-element.108), channel_id=1, source_target_pairs={{0,4},{4,8},{8,12},{12,16},{16,20},{20,24},{24,28},{1,5},{5,9},{9,... | collective-permute-start | bytes 57608 | tf_op jit(solution)/shard_map/ppermute | solution.py:23
  114.3 20.5 %collective-permute-start.9 = (bf16[75,1,64]{0,2,1:T(8,128)(2,1)S(1)}, bf16[75,1,64]{0,2,1:T(8,128)(2,1)S(1)}, u32[]{:S(2)}, u32[]{:S(2)}) collective-permute-start(bf16[75,1,64]{0,2,1:T(8,128)(2,1)S(1)} %get-tuple-element.177), channel_id=1, source_target_pairs={{4,0},{8,4},{12,8},{16,12},{20,16},{24,20},{28,24},{5,1},{9,5},{13... | collective-permute-start | bytes 28808 | tf_op jit(solution)/shard_map/ppermute | solution.py:24
  115.6 20.7 %collective-permute-start.8 = (bf16[75,1,64]{0,2,1:T(8,128)(2,1)S(1)}, bf16[75,1,64]{0,2,1:T(8,128)(2,1)S(1)}, u32[]{:S(2)}, u32[]{:S(2)}) collective-permute-start(bf16[75,1,64]{0,2,1:T(8,128)(2,1)S(1)} %get-tuple-element.176), channel_id=1, source_target_pairs={{0,4},{4,8},{8,12},{12,16},{16,20},{20,24},{24,28},{1,5},{5,9},{9,... | collective-permute-start | bytes 28808 | tf_op jit(solution)/shard_map/ppermute | solution.py:23
  141.5 18.2 %collective-permute-start.13 = (bf16[75,1,64]{0,2,1:T(8,128)(2,1)S(1)}, bf16[75,1,64]{0,2,1:T(8,128)(2,1)S(1)}, u32[]{:S(2)}, u32[]{:S(2)}) collective-permute-start(bf16[75,1,64]{0,2,1:T(8,128)(2,1)S(1)} %get-tuple-element.175), channel_id=1, source_target_pairs={{4,0},{8,4},{12,8},{16,12},{20,16},{24,20},{28,24},{5,1},{9,5},{13... | collective-permute-start | bytes 28808 | tf_op jit(solution)/shard_map/ppermute | solution.py:24
  142.8 18.3 %collective-permute-start.12 = (bf16[75,1,64]{0,2,1:T(8,128)(2,1)S(1)}, bf16[75,1,64]{0,2,1:T(8,128)(2,1)S(1)}, u32[]{:S(2)}, u32[]{:S(2)}) collective-permute-start(bf16[75,1,64]{0,2,1:T(8,128)(2,1)S(1)} %get-tuple-element.174), channel_id=1, source_target_pairs={{0,4},{4,8},{8,12},{12,16},{16,20},{20,24},{24,28},{1,5},{5,9},{9,... | collective-permute-start | bytes 28808 | tf_op jit(solution)/shard_map/ppermute | solution.py:23
  169.4 7.2 collective-permute-start.17
  218.4 7.2 collective-permute-start.28
  233.1 7.2 collective-permute-start.32
  263.4 7.3 collective-permute-start.40
  270.7 8.0 collective-permute-start.43
  392.2 16.7 %collective-permute-start.51 = (bf16[75,6,1]{0,2,1:T(2,128)(2,1)S(1)}, bf16[75,6,1]{0,2,1:T(2,128)(2,1)S(1)}, u32[]{:S(2)}, u32[]{:S(2)}) collective-permute-start(bf16[75,6,1]{0,2,1:T(2,128)(2,1)S(1)} %get-tuple-element.77), channel_id=1, source_target_pairs={{1,0},{2,1},{3,2},{5,4},{6,5},{7,6},{9,8},{10,9},{11,10},{13,12},{... | collective-permute-start | bytes 2708 | tf_op jit(solution)/shard_map/ppermute | solution.py:24
  393.5 15.4 %collective-permute-start.50 = (bf16[75,6,1]{0,2,1:T(2,128)(2,1)S(1)}, bf16[75,6,1]{0,2,1:T(2,128)(2,1)S(1)}, u32[]{:S(2)}, u32[]{:S(2)}) collective-permute-start(bf16[75,6,1]{0,2,1:T(2,128)(2,1)S(1)} %get-tuple-element.76), channel_id=1, source_target_pairs={{0,1},{1,2},{2,3},{4,5},{5,6},{6,7},{8,9},{9,10},{10,11},{12,13},{... | collective-permute-start | bytes 2708 | tf_op jit(solution)/shard_map/ppermute | solution.py:23
  410.6 7.2 collective-permute-start.52
  425.7 7.2 collective-permute-start.56
  457.8 7.2 collective-permute-start.65
  488.5 7.2 collective-permute-start.72
  532.2 15.1 %collective-permute-start.85 = (bf16[75,1,128]{0,2,1:T(8,128)(2,1)S(1)}, bf16[75,1,128]{0,2,1:T(8,128)(2,1)S(1)}, u32[]{:S(2)}, u32[]{:S(2)}) collective-permute-start(bf16[75,1,128]{0,2,1:T(8,128)(2,1)S(1)} %get-tuple-element.97), channel_id=1, source_target_pairs={{4,0},{8,4},{12,8},{16,12},{20,16},{24,20},{28,24},{5,1},{9,5},{13... | collective-permute-start | bytes 57608 | tf_op jit(solution)/shard_map/ppermute | solution.py:24
  533.5 13.8 %collective-permute-start.84 = (bf16[75,1,128]{0,2,1:T(8,128)(2,1)S(1)}, bf16[75,1,128]{0,2,1:T(8,128)(2,1)S(1)}, u32[]{:S(2)}, u32[]{:S(2)}) collective-permute-start(bf16[75,1,128]{0,2,1:T(8,128)(2,1)S(1)} %get-tuple-element.96), channel_id=1, source_target_pairs={{0,4},{4,8},{8,12},{12,16},{16,20},{20,24},{24,28},{1,5},{5,9},{9,... | collective-permute-start | bytes 57608 | tf_op jit(solution)/shard_map/ppermute | solution.py:23
  547.3 18.0 %collective-permute-start.87 = (bf16[75,6,1]{0,2,1:T(2,128)(2,1)S(1)}, bf16[75,6,1]{0,2,1:T(2,128)(2,1)S(1)}, u32[]{:S(2)}, u32[]{:S(2)}) collective-permute-start(bf16[75,6,1]{0,2,1:T(2,128)(2,1)S(1)} %get-tuple-element.73), channel_id=1, source_target_pairs={{1,0},{2,1},{3,2},{5,4},{6,5},{7,6},{9,8},{10,9},{11,10},{13,12},{... | collective-permute-start | bytes 2708 | tf_op jit(solution)/shard_map/ppermute | solution.py:24
  548.6 16.7 %collective-permute-start.86 = (bf16[75,6,1]{0,2,1:T(2,128)(2,1)S(1)}, bf16[75,6,1]{0,2,1:T(2,128)(2,1)S(1)}, u32[]{:S(2)}, u32[]{:S(2)}) collective-permute-start(bf16[75,6,1]{0,2,1:T(2,128)(2,1)S(1)} %get-tuple-element.72), channel_id=1, source_target_pairs={{0,1},{1,2},{2,3},{4,5},{5,6},{6,7},{8,9},{9,10},{10,11},{12,13},{... | collective-permute-start | bytes 2708 | tf_op jit(solution)/shard_map/ppermute | solution.py:23
  646.8 7.2 collective-permute-start.96
  661.7 7.2 collective-permute-start.100
  762.8 7.9 collective-permute-start.127
  772.6 15.1 %collective-permute-start.129 = (bf16[75,1,128]{0,2,1:T(8,128)(2,1)S(1)}, bf16[75,1,128]{0,2,1:T(8,128)(2,1)S(1)}, u32[]{:S(2)}, u32[]{:S(2)}) collective-permute-start(bf16[75,1,128]{0,2,1:T(8,128)(2,1)S(1)} %get-tuple-element.89), channel_id=1, source_target_pairs={{4,0},{8,4},{12,8},{16,12},{20,16},{24,20},{28,24},{5,1},{9,5},{13... | collective-permute-start | bytes 57608 | tf_op jit(solution)/shard_map/ppermute | solution.py:24
  773.9 13.8 %collective-permute-start.128 = (bf16[75,1,128]{0,2,1:T(8,128)(2,1)S(1)}, bf16[75,1,128]{0,2,1:T(8,128)(2,1)S(1)}, u32[]{:S(2)}, u32[]{:S(2)}) collective-permute-start(bf16[75,1,128]{0,2,1:T(8,128)(2,1)S(1)} %get-tuple-element.88), channel_id=1, source_target_pairs={{0,4},{4,8},{8,12},{12,16},{16,20},{20,24},{24,28},{1,5},{5,9},{9,... | collective-permute-start | bytes 57608 | tf_op jit(solution)/shard_map/ppermute | solution.py:23
  787.7 19.6 %collective-permute-start.131 = (bf16[75,6,1]{0,2,1:T(2,128)(2,1)S(1)}, bf16[75,6,1]{0,2,1:T(2,128)(2,1)S(1)}, u32[]{:S(2)}, u32[]{:S(2)}) collective-permute-start(bf16[75,6,1]{0,2,1:T(2,128)(2,1)S(1)} %get-tuple-element.65), channel_id=1, source_target_pairs={{1,0},{2,1},{3,2},{5,4},{6,5},{7,6},{9,8},{10,9},{11,10},{13,12},{... | collective-permute-start | bytes 2708 | tf_op jit(solution)/shard_map/ppermute | solution.py:24
  789.0 18.3 %collective-permute-start.130 = (bf16[75,6,1]{0,2,1:T(2,128)(2,1)S(1)}, bf16[75,6,1]{0,2,1:T(2,128)(2,1)S(1)}, u32[]{:S(2)}, u32[]{:S(2)}) collective-permute-start(bf16[75,6,1]{0,2,1:T(2,128)(2,1)S(1)} %get-tuple-element.64), channel_id=1, source_target_pairs={{0,1},{1,2},{2,3},{4,5},{5,6},{6,7},{8,9},{9,10},{10,11},{12,13},{... | collective-permute-start | bytes 2708 | tf_op jit(solution)/shard_map/ppermute | solution.py:23
  879.9 113.0 %all-to-all-start.1 = ((bf16[64,75,4,128]{3,2,1,0:T(4,128)(2,1)}), bf16[64,75,4,128]{3,2,1,0:T(4,128)(2,1)}, u32[]{:S(2)}, u32[]{:S(2)}) async-start(bf16[64,75,4,128]{3,2,1,0:T(4,128)(2,1)} %reshape.181), calls=%async_computation.1 | async-start | bytes 9830400 | tf_op jit(solution)/shard_map/all_to_all | solution.py:135
  (114 other events, 1221.1 us)
where the time goes:
time: 1010 us; the launch traced here: 999 us
  starting transfers between devices  486 us (48%)
  waiting for transfers between devices  226 us (22%)
  blocking collectives  140 us (14%)
  local copies, waits for them, and re-layouts  52.1 us (5%)
  other arithmetic  42.8 us (4%)
  matrix products  38.9 us (4%)
  between operations  13.2 us (1%)
    ppermute x66, starting transfers between devices, with_halo(): before = lax.ppermute(last, axis, up)  387 us
    psum x3, blocking collectives, merged(): lax.psum((jnp.sum(residual * residual), jnp.sum(residual * image)), ('ens...  140 us
    all_to_all x1, waiting for transfers between devices, local(): lax.all_to_all(final, ('ens', 'gx'), split_axis=0, concat_axis=2, tiled=T...  107 us
    ppermute x66, starting transfers between devices, with_halo(): after = lax.ppermute(leading, axis, down)  85.8 us
    ppermute x66, waiting for transfers between devices, with_halo(): before = lax.ppermute(last, axis, up)  81 us
    dot_general x4, matrix products, member_products(): jnp.einsum('ij,kjc->kic', spread, flat, preferred_element_type=jnp.float32)  38.9 us
    ppermute x66, waiting for transfers between devices, with_halo(): after = lax.ppermute(leading, axis, down)  38.5 us
    convert_element_type x4, other arithmetic, member_products(): product = (tiles * masked).astype(jnp.bfloat16)  27.1 us
  transfers between devices with their start and end apart: 134, of which 60 were waited for; matrix products, arithmetic and copies ran while one was open for 5% of the time, Pallas kernels for 0%

commit v1 on v0

v1 whole, which is shorter than its diff:
```python
import functools

import jax
import jax.numpy as jnp
from jax import lax
from jax.experimental import pallas as pl
from jax.experimental.pallas import tpu as pltpu
from jax.sharding import PartitionSpec as P

GRIDS = 3
SWEEPS = 2
COARSE_SWEEPS = 4
ITERATIONS = 3
SUB = 8
LANES = 128

diffusivity = 16.0
damping = 0.8
MESH = pl.DeviceIdType.MESH
F32 = jnp.float32
BF16 = jnp.bfloat16


def strength_of(level):
    return diffusivity / 4.0**level


def lane_index(width):
    return lax.broadcasted_iota(jnp.int32, (SUB, width), 1)


def over_rows(count, body):
    chunk = min(SUB, count)

    @pl.loop(0, count // chunk)
    def _(block):
        start = block * chunk
        for row in range(chunk):
            body(start + row)


def neighbours(ref, row, step):
    here = ref[row + 1]
    width = here.shape[-1]
    lane = lane_index(width)
    left = jnp.where(lane < step, 0.0, pltpu.roll(here, step, 1))
    right = jnp.where(lane >= width - step, 0.0, pltpu.roll(here, width - step, 1))
    return here, ref[row] + ref[row + 2] + left + right


def relax(src, source, dst, rows, level, scale=None):
    strength = strength_of(level)
    factor = damping / (1.0 + 4.0 * strength)

    def body(row):
        here, around = neighbours(src, row, 2**level)
        if scale is not None:
            here, around = here * scale, around * scale
        dst[row + 1] = (1.0 - damping) * here + factor * (source[row + 1] + strength * around)

    over_rows(rows, body)


def restrict_remainder(src, source, dst, rows, level):
    strength = strength_of(level)
    step = 2**level

    def one(row):
        here, around = neighbours(src, row, step)
        left_over = source[row + 1] - (1.0 + 4.0 * strength) * here + strength * around
        return left_over

    def body(row):
        both = one(2 * row) + one(2 * row + 1)
        width = both.shape[-1]
        even = lax.rem(lane_index(width) // step, 2) == 0
        other = jnp.where(even, pltpu.roll(both, width - step, 1), pltpu.roll(both, step, 1))
        dst[row + 1] = 0.25 * (both + other)

    over_rows(rows // 2, body)


def add_prolonged(dst, coarse, rows):
    def body(row):
        extra = coarse[row + 1]
        dst[2 * row + 1] = dst[2 * row + 1] + extra
        dst[2 * row + 2] = dst[2 * row + 2] + extra

    over_rows(rows // 2, body)


def vcycle(levels, level, rows):
    source, first, second = levels[level]
    factor = damping / (1.0 + 4.0 * strength_of(level))
    if level == GRIDS - 1:
        relax(source, source, first, rows, level, factor)
        for _ in range(COARSE_SWEEPS - 2):
            relax(first, source, second, rows, level)
            first, second = second, first
        return first
    relax(source, source, first, rows, level, factor)
    for _ in range(SWEEPS - 2):
        relax(first, source, second, rows, level)
        first, second = second, first
    restrict_remainder(first, source, levels[level + 1][0], rows, level)
    coarse = vcycle(levels, level + 1, rows // 2)
    add_prolonged(first, coarse, rows)
    for _ in range(SWEEPS):
        relax(first, source, second, rows, level)
        first, second = second, first
    return first


def kernel(
    sizes,
    groups,
    members,
    spread,
    sea,
    innovations,
    obs_error,
    scale,
    increment,
    alpha_fields,
    tiles,
    gathered,
    w_send,
    residual,
    direction,
    along,
    cov_dir,
    weights,
    cov_res,
    image,
    f_send,
    back,
    p_send,
    p_recv,
    f_recv,
    f_along,
    *rest,
):
    n_ens, n_gx, n_gy = sizes
    level_refs = rest[: 3 * GRIDS]
    (m_ssem, m_rsem, f_ssem, f_rsem, b_ssem, b_rsem, p_ssem, p_rsem, w_ssem, w_rsem) = rest[3 * GRIDS :]
    levels = [level_refs[3 * g : 3 * g + 3] for g in range(GRIDS)]
    f_res = levels[0][0]
    n_blocks = n_ens * n_gx
    n_dev = n_blocks * n_gy
    spacing = n_dev // groups
    block = lax.axis_index("ens") * n_gx + lax.axis_index("gx")
    column = lax.axis_index("gy")
    me = block * n_gy + column
    is_owner = (lax.rem(me, spacing) == 0) & (me // spacing < groups)
    my_group = jnp.minimum(me // spacing, groups - 1)
    tile_rows = innovations.shape[0]
    per_block = members.shape[1]
    grid_rows = tile_rows * n_blocks

    def device(rank):
        return (rank // (n_gx * n_gy), lax.rem(rank // n_gy, n_gx), lax.rem(rank, n_gy))

    def group_rows(group):
        return pl.ds(pl.multiple_of(group * SUB, SUB), SUB)

    def grid_slot(ref, rank):
        rows = pl.ds((rank // n_gy) * tile_rows + 1, tile_rows)
        lanes = pl.ds(pl.multiple_of(lax.rem(rank, n_gy) * LANES, LANES), LANES)
        return ref.at[rows, :, lanes]

    def send(src, dst, send_sem, recv_sem, rank):
        @pl.when(rank == me)
        def _():
            pltpu.make_async_copy(src, dst, recv_sem).start()

        @pl.when(rank != me)
        def _():
            pltpu.make_async_remote_copy(
                src_ref=src,
                dst_ref=dst,
                send_sem=send_sem,
                recv_sem=recv_sem,
                device_id=device(rank),
                device_id_type=MESH,
            ).start()

    def sent(src, send_sem, rank):
        @pl.when(rank != me)
        def _():
            pltpu.make_async_copy(src, src, send_sem).wait()

    def arrived(dst, recv_sem):
        pltpu.make_async_copy(dst, dst, recv_sem).wait()

    barrier = pltpu.get_barrier_semaphore()

    @pl.loop(1, n_dev)
    def _(step):
        pl.semaphore_signal(
            barrier, inc=1, device_id=device(lax.rem(me + step, n_dev)), device_id_type=MESH
        )

    for r in range(tile_rows):
        start = innovations[r]
        residual[r] = start
        f_send[r] = scale[r] * (sea[r] * start)
        zero = jnp.zeros_like(start)
        for ref in (direction, along, cov_dir, weights):
            ref[r] = zero
        increment[r] = zero

    @pl.when(is_owner)
    def _():
        for source, first, second in levels:
            for ref in (source, first, second):
                edge = jnp.zeros(ref.shape[1:], F32)
                ref[0] = edge
                ref[ref.shape[0] - 1] = edge

        def clear(row):
            f_along[row + 1] = jnp.zeros(f_along.shape[1:], F32)
            f_res[row + 1] = jnp.zeros(f_res.shape[1:], F32)

        over_rows(grid_rows, clear)

    pl.semaphore_wait(barrier, n_dev - 1)

    def send_source():
        @pl.loop(0, groups)
        def _(group):
            send(
                f_send.at[:, group_rows(group), :],
                grid_slot(f_recv, me),
                f_ssem.at[group],
                f_rsem.at[me],
                group * spacing,
            )

    def source_sent():
        @pl.loop(0, groups)
        def _(group):
            sent(f_send.at[:, group_rows(group), :], f_ssem.at[group], group * spacing)

    send_source()

    @pl.loop(0, n_blocks)
    def _(step):
        target = lax.rem(block + step, n_blocks)
        send(
            members.at[target],
            tiles.at[block],
            m_ssem.at[target],
            m_rsem.at[block],
            target * n_gy + column,
        )

    def mix(values, vector):
        product = [
            (values[r].astype(F32) * vector[r]).astype(BF16) for r in range(tile_rows)
        ]
        mixed = jnp.dot(
            spread[...], jnp.concatenate(product, axis=1), preferred_element_type=F32
        )
        return [mixed[:, r * LANES : (r + 1) * LANES] for r in range(tile_rows)]

    def iterate(iteration, carry):
        alpha, ratio, norm = carry

        @pl.when(is_owner)
        def _():
            @pl.loop(0, n_dev)
            def _(rank):
                arrived(grid_slot(f_recv, rank), f_rsem.at[rank])

            def advance(row):
                new = f_recv[row + 1] + ratio * f_along[row + 1]
                f_along[row + 1] = new
                f_res[row + 1] = f_res[row + 1] - alpha * new

            over_rows(grid_rows, advance)
            result = vcycle(levels, 0, grid_rows)

            @pl.loop(0, n_dev)
            def _(rank):
                send(
                    grid_slot(result, rank),
                    back.at[:, group_rows(my_group), :],
                    b_ssem.at[rank],
                    b_rsem.at[my_group],
                    rank,
                )

        for r in range(tile_rows):
            image[r] = sea[r] * residual[r]
            cov_res[r] = jnp.zeros_like(image[r])

        @pl.loop(0, n_blocks)
        def _(step):
            origin = lax.rem(block - step + n_blocks, n_blocks)

            @pl.when(iteration == 0)
            def _():
                arrived(tiles.at[origin], m_rsem.at[origin])

            @pl.loop(0, per_block)
            def _(k):
                values = tiles[origin, k]
                mixed = mix(values, image)
                for r in range(tile_rows):
                    cov_res[r] = cov_res[r] + values[r].astype(F32) * mixed[r]

        @pl.loop(0, groups)
        def _(group):
            arrived(back.at[:, group_rows(group), :], b_rsem.at[group])

        source_sent()
        own = jnp.zeros((1, LANES), F32)
        cross = jnp.zeros((1, LANES), F32)
        for r in range(tile_rows):
            cov = sea[r] * (cov_res[r] + scale[r] * back[r])
            now = residual[r]
            img = cov + obs_error[r] * now
            cov_res[r] = cov
            image[r] = img
            f_send[r] = scale[r] * (sea[r] * img)
            own = own + jnp.sum(now * now, axis=0, keepdims=True)
            cross = cross + jnp.sum(now * img, axis=0, keepdims=True)
        p_send[iteration, 0:1] = own
        p_send[iteration, 1:2] = cross

        @pl.loop(0, n_dev)
        def _(step):
            rank = lax.rem(me + step, n_dev)
            send(
                p_send.at[iteration],
                p_recv.at[iteration, me],
                p_ssem.at[iteration, rank],
                p_rsem.at[iteration, me],
                rank,
            )

        @pl.when(iteration < ITERATIONS - 1)
        def _():
            send_source()

        @pl.loop(0, n_dev)
        def _(rank):
            arrived(p_recv.at[iteration, rank], p_rsem.at[iteration, rank])

        total = jnp.sum(jnp.sum(p_recv[iteration], axis=0), axis=1, keepdims=True)
        norm_next, product = total[0:1], total[1:2]
        ratio = jnp.where(iteration == 0, 0.0, norm_next / norm)
        alpha = norm_next / (product - ratio * norm_next / alpha)
        for r in range(tile_rows):
            step_to = residual[r] + ratio * direction[r]
            direction[r] = step_to
            weights[r] = weights[r] + alpha * step_to
            cov = cov_res[r] + ratio * cov_dir[r]
            cov_dir[r] = cov
            increment[r] = increment[r] + alpha * cov
            img = image[r] + ratio * along[r]
            along[r] = img
            residual[r] = residual[r] - alpha * img

        @pl.loop(0, n_dev)
        def _(rank):
            sent(p_send.at[iteration], p_ssem.at[iteration, rank], rank)

        @pl.when(is_owner)
        def _():
            @pl.loop(0, n_dev)
            def _(rank):
                sent(grid_slot(levels[0][1], rank), b_ssem.at[rank], rank)

        return alpha, ratio, norm_next

    one = jnp.ones((1, 1), F32)
    lax.fori_loop(0, ITERATIONS, iterate, (-one, one * 0.0, one))

    for r in range(tile_rows):
        w_send[r] = (sea[r] * weights[r]).astype(BF16)

    @pl.loop(0, n_blocks)
    def _(step):
        target = lax.rem(block + step, n_blocks)
        send(
            w_send,
            gathered.at[block],
            w_ssem.at[target],
            w_rsem.at[block],
            target * n_gy + column,
        )

    @pl.loop(0, n_blocks)
    def _(step):
        origin = lax.rem(block - step + n_blocks, n_blocks)
        arrived(gathered.at[origin], w_rsem.at[origin])
        for r in range(tile_rows):
            image[r] = gathered[origin, r].astype(F32)

        @pl.loop(0, per_block)
        def _(k):
            mixed = mix(members[origin, k], image)
            for r in range(tile_rows):
                alpha_fields[k, origin, r] = mixed[r].astype(BF16)

    @pl.loop(0, n_blocks)
    def _(target):
        sent(w_send, w_ssem.at[target], target * n_gy + column)
        sent(members.at[target], m_ssem.at[target], target * n_gy + column)


def local(sizes, members, spread, sea_mask, innovations, obs_error, static_scale):
    n_ens, n_gx, n_gy = sizes
    n_blocks = n_ens * n_gx
    n_dev = n_blocks * n_gy
    count, layers, rows, lanes = members.shape
    tile_rows = innovations.shape[1]
    groups = -(-layers // SUB)
    padded = groups * SUB
    extra = padded - layers
    grid_rows = rows
    width = lanes * n_gy

    by_row = members.reshape(count, layers, n_blocks, tile_rows, lanes).transpose(2, 0, 3, 1, 4)
    by_row = jnp.pad(by_row, ((0, 0), (0, 0), (0, 0), (0, extra), (0, 0)))

    def field(values):
        return jnp.pad(values.transpose(1, 0, 2), ((0, 0), (0, extra), (0, 0)))

    sea = sea_mask.astype(F32)[:, None, :]
    spread = jnp.pad(spread, ((0, extra), (0, extra)))
    tile = (tile_rows, padded, lanes)
    f_tile = pltpu.VMEM(tile, F32)
    scratch = [
        pltpu.VMEM((n_blocks, count, *tile), BF16),
        pltpu.VMEM((n_blocks, *tile), BF16),
        pltpu.VMEM(tile, BF16),
    ]
    scratch += [f_tile] * 9
    scratch += [
        pltpu.VMEM((ITERATIONS, 2, lanes), F32),
        pltpu.VMEM((ITERATIONS, n_dev, 2, lanes), F32),
        pltpu.VMEM((grid_rows + 2, SUB, width), F32),
        pltpu.VMEM((grid_rows + 2, SUB, width), F32),
    ]
    for level in range(GRIDS):
        scratch += [pltpu.VMEM((grid_rows // 2**level + 2, SUB, width), F32)] * 3
    dma = pltpu.SemaphoreType.DMA
    scratch += [
        dma((n_blocks,)),
        dma((n_blocks,)),
        dma((groups,)),
        dma((n_dev,)),
        dma((n_dev,)),
        dma((groups,)),
        dma((ITERATIONS, n_dev)),
        dma((ITERATIONS, n_dev)),
        dma((n_blocks,)),
        dma((n_blocks,)),
    ]
    vmem = pl.BlockSpec(memory_space=pltpu.VMEM)
    increment, alpha_fields = pl.pallas_call(
        functools.partial(kernel, sizes, groups),
        out_shape=(
            jax.ShapeDtypeStruct(tile, F32),
            jax.ShapeDtypeStruct((count, n_blocks, *tile), BF16),
        ),
        in_specs=[vmem] * 6,
        out_specs=(vmem, vmem),
        scratch_shapes=scratch,
        compiler_params=pltpu.CompilerParams(
            collective_id=0, has_side_effects=True, vmem_limit_bytes=60 * 2**20
        ),
        name="window",
    )(by_row, spread, sea, field(innovations), field(obs_error), field(static_scale))
    increment = increment[:, :layers].transpose(1, 0, 2)
    alpha_fields = alpha_fields.reshape(count, rows, padded, lanes)[:, :, :layers]
    return increment, alpha_fields.transpose(0, 2, 1, 3)


def solution(mesh):
    in_specs = (
        P(("ens", "gx"), None, None, "gy"),
        P(),
        P(("ens", "gx"), "gy"),
        P(None, ("ens", "gx"), "gy"),
        P(None, ("ens", "gx"), "gy"),
        P(None, ("ens", "gx"), "gy"),
    )
    out_specs = (P(None, ("ens", "gx"), "gy"), P(("ens", "gx"), None, None, "gy"))
    sizes = tuple(mesh.shape[axis] for axis in ("ens", "gx", "gy"))
    return jax.shard_map(
        functools.partial(local, sizes),
        mesh=mesh,
        in_specs=in_specs,
        out_specs=out_specs,
        check_vma=False,
    )
```

time: 1010 us -> 235 us (0.23)
  starting transfers between devices: 486 us -> 0 us
  waiting for transfers between devices: 226 us -> 0 us
  Pallas kernels: 0 us -> 209 us
  blocking collectives: 140 us -> 0 us
  other arithmetic: 42.8 us -> 1.22 us
  matrix products: 38.9 us -> 0 us
  local copies, waits for them, and re-layouts: 52.1 us -> 23.2 us
  between operations: 13.2 us -> 0.66 us
    ppermute x132 -> x0, starting transfers between devices: 473 us -> none  [the longest x66 387 us: with_halo(): before = lax.ppermute(last, axis, up)]
    pallas_call x0 -> x1, Pallas kernels: none -> 209 us  [local(): pl.pallas_call(functools.partial(kernel, sizes, groups), out_shape=(jax.S...]
    psum x3 -> x0, blocking collectives: 140 us -> none  [merged(): lax.psum((jnp.sum(residual * residual), jnp.sum(residual * image)), ('ens...]
    ppermute x132 -> x0, waiting for transfers between devices: 119 us -> none  [the longest x66 81 us: with_halo(): before = lax.ppermute(last, axis, up)]
    all_to_all x2 -> x0, waiting for transfers between devices: 107 us -> none  [the longest x1 107 us: local(): lax.all_to_all(final, ('ens', 'gx'), split_axis=0, concat_axis=2, tiled=T...]
    dot_general x4 -> x0, matrix products: 38.9 us -> none  [member_products(): jnp.einsum('ij,kjc->kic', spread, flat, preferred_element_type=jnp.float32)]
    convert_element_type x53 -> x1, other arithmetic: 34.6 us -> 1.22 us  [local(): sea = sea_mask.astype(F32)[:, None, :]]
    convert_element_type x3 -> x0, local copies, waits for them, and re-layouts: 31 us -> none  [the longest x2 21.7 us: covariance(): ensemble = jnp.sum(tiles * mixed, axis=0)]
  transfers between devices with their start and end apart: 134 -> 0, of which waited for: 60 -> 0; matrix products, arithmetic and copies ran while one was open for 5% -> 0% of each run, Pallas kernels for 0% -> 0%
where the time goes in v1:
time: 235 us; the launch traced here: 234 us
  Pallas kernels  209 us (89%)
  local copies, waits for them, and re-layouts  23.2 us (10%)
    pallas_call x1, Pallas kernels, local(): pl.pallas_call(functools.partial(kernel, sizes, groups), out_shape=(jax.S...  209 us
    unnamed x5, local copies, waits for them, and re-layouts  9.5 us
    reshape x1, local copies, waits for them, and re-layouts, local(): members.reshape(count, layers, n_blocks, tile_rows, lanes)  5.56 us

profile of v1, /device:TPU:0, one launch (start us, length us, event | category | flops | bytes accessed | tf_op | source)
XLA Modules:
  0.0 233.6 jit_solution(15044618122726270150)
XLA Ops:
  0.6 1.2 convert_element_type.11
  1.8 1.3 pad.19.spread
  3.2 0.9 copy.32
  4.1 0.7 pad.20.innovations
  4.8 0.9 copy.31
  5.7 0.7 pad.21.obs_error
  6.4 0.9 copy.30
  7.3 0.7 pad.22.scale
  8.0 5.6 %copy.28 = bf16[8,75,8,4,128]{4,1,3,0,2:T(8,128)(2,1)S(1)} copy(bf16[8,75,8,4,128]{4,3,2,1,0:T(4,128)(2,1)} %bitcast.23) | data formatting | bytes 9830400 | tf_op jit(solution)/shard_map/reshape | solution.py:425
  13.6 3.8 %pad.18.members = bf16[8,8,4,80,128]{4,3,2,1,0:T(8,128)(2,1)} pad(bf16[8,8,4,75,128]{4,3,2,1,0:T(8,128)(2,1)S(1)} %bitcast.21, bf16[]{:T(256)} %constant.3.clone.1), padding=0_0x0_0x0_0x0_5x0_0 | pad | bytes 10158082 | tf_op jit(solution)/shard_map/jit(_pad)/pad | solution.py:426
  17.4 208.6 %window.1 = (f32[4,80,128]{2,1,0:T(8,128)}, bf16[8,8,4,80,128]{4,3,2,1,0:T(8,128)(2,1)}) custom-call(bf16[8,8,4,80,128]{4,3,2,1,0:T(8,128)(2,1)} %pad.18.members, bf16[80,80]{1,0:T(8,128)(2,1)} %pad.19.spread, f32[4,1,128]{2,1,0:T(1,128)} %bitcast.28, f32[4,80,128]{2,1,0:T(8,128)} %pad.20.innovations, f32[4,80,128]{2,1,0:T(8,128)} %pad.21.obs_error, ...), custom_call_target="tpu_custom_call" | custom-call | tf_op jit(solution)/shard_map/window/pallas_call | solution.py:463
  225.9 0.9 slice_bitcast_fusion
  226.9 0.7 copy.19
  227.6 6.0 %copy.29 = bf16[8,32,75,128]{3,1,2,0:T(8,128)(2,1)} copy(bf16[8,32,75,128]{3,2,1,0:T(8,128)(2,1)} %bitcast.22) | data formatting | bytes 9830400

commit v2 on v1

--- a/solution.py
+++ b/solution.py
@@ -122,29 +122,27 @@
     scale,
     increment,
     alpha_fields,
-    tiles,
     gathered,
-    w_send,
+    r_send,
+    s_recv,
     residual,
-    direction,
     along,
     cov_dir,
-    weights,
     cov_res,
+    total,
     image,
     f_send,
     back,
     p_send,
     p_recv,
-    f_recv,
     f_along,
     *rest,
 ):
     n_ens, n_gx, n_gy = sizes
     level_refs = rest[: 3 * GRIDS]
-    (m_ssem, m_rsem, f_ssem, f_rsem, b_ssem, b_rsem, p_ssem, p_rsem, w_ssem, w_rsem) = rest[3 * GRIDS :]
+    (f_ssem, f_rsem, b_ssem, b_rsem, p_ssem, p_rsem, r_ssem, r_rsem, s_ssem, s_rsem) = rest[3 * GRIDS :]
     levels = [level_refs[3 * g : 3 * g + 3] for g in range(GRIDS)]
-    f_res = levels[0][0]
+    f_res, f_recv = levels[0][0], levels[0][2]
     n_blocks = n_ens * n_gx
     n_dev = n_blocks * n_gy
     spacing = n_dev // groups
@@ -154,7 +152,8 @@
     is_owner = (lax.rem(me, spacing) == 0) & (me // spacing < groups)
     my_group = jnp.minimum(me // spacing, groups - 1)
     tile_rows = innovations.shape[0]
-    per_block = members.shape[1]
+    layers = innovations.shape[1]
+    count = members.shape[0]
     grid_rows = tile_rows * n_blocks
 
     def device(rank):
@@ -203,11 +202,12 @@
     for r in range(tile_rows):
         start = innovations[r]
         residual[r] = start
-        f_send[r] = scale[r] * (sea[r] * start)
+        f_send[r] = jnp.zeros(f_send.shape[1:], F32)
+        f_send[r, :layers] = scale[r] * (sea[r] * start)
+        r_send[r] = (sea[r] * start).astype(BF16)
         zero = jnp.zeros_like(start)
-        for ref in (direction, along, cov_dir, weights):
+        for ref in (along, cov_dir, increment):
             ref[r] = zero
-        increment[r] = zero
 
     @pl.when(is_owner)
     def _():
@@ -241,18 +241,28 @@
         def _(group):
             sent(f_send.at[:, group_rows(group), :], f_ssem.at[group], group * spacing)
 
+    def part_of(origin):
+        return alpha_fields.at[0, pl.ds(origin * tile_rows, tile_rows)]
+
+    def send_residual(iteration):
+        @pl.loop(0, n_blocks)
+        def _(step):
+            target = lax.rem(block + step, n_blocks)
+            send(
+                r_send,
+                gathered.at[iteration, block],
+                r_ssem.at[target],
+                r_rsem.at[iteration, block],
+                target * n_gy + column,
+            )
+
+    def residual_sent():
+        @pl.loop(0, n_blocks)
+        def _(target):
+            sent(r_send, r_ssem.at[target], target * n_gy + column)
+
     send_source()
-
-    @pl.loop(0, n_blocks)
-    def _(step):
-        target = lax.rem(block + step, n_blocks)
-        send(
-            members.at[target],
-            tiles.at[block],
-            m_ssem.at[target],
-            m_rsem.at[block],
-            target * n_gy + column,
-        )
+    send_residual(0)
 
     def mix(values, vector):
         product = [
@@ -264,7 +274,7 @@
         return [mixed[:, r * LANES : (r + 1) * LANES] for r in range(tile_rows)]
 
     def iterate(iteration, carry):
-        alpha, ratio, norm = carry
+        alpha, ratio, norm, along_terms, weight_terms = carry
 
         @pl.when(is_owner)
         def _():
@@ -290,24 +300,44 @@
                     rank,
                 )
 
-        for r in range(tile_rows):
-            image[r] = sea[r] * residual[r]
-            cov_res[r] = jnp.zeros_like(image[r])
-
         @pl.loop(0, n_blocks)
         def _(step):
             origin = lax.rem(block - step + n_blocks, n_blocks)
-
-            @pl.when(iteration == 0)
-            def _():
-                arrived(tiles.at[origin], m_rsem.at[origin])
-
-            @pl.loop(0, per_block)
+            arrived(gathered.at[iteration, origin], r_rsem.at[iteration, origin])
+            for r in range(tile_rows):
+                image[r] = gathered[iteration, origin, r].astype(F32)
+                total[r] = jnp.zeros_like(total[r])
+
+            @pl.loop(0, count)
             def _(k):
-                values = tiles[origin, k]
+                values = [members[k, origin * tile_rows + r] for r in range(tile_rows)]
                 mixed = mix(values, image)
                 for r in range(tile_rows):
-                    cov_res[r] = cov_res[r] + values[r].astype(F32) * mixed[r]
+                    total[r] = total[r] + values[r].astype(F32) * mixed[r]
+
+            @pl.when(step == 0)
+            def _():
+                for r in range(tile_rows):
+                    cov_res[r] = total[r]
+
+            @pl.when(step > 0)
+            def _():
+                for r in range(tile_rows):
+                    alpha_fields[0, origin * tile_rows + r] = total[r].astype(BF16)
+                send(
+                    part_of(origin),
+                    s_recv.at[block],
+                    s_ssem.at[origin],
+                    s_rsem.at[block],
+                    origin * n_gy + column,
+                )
+
+        @pl.loop(1, n_blocks)
+        def _(step):
+            origin = lax.rem(block - step + n_blocks, n_blocks)
+            arrived(s_recv.at[origin], s_rsem.at[origin])
+            for r in range(tile_rows):
+                cov_res[r] = cov_res[r] + s_recv[origin, r].astype(F32)
 
         @pl.loop(0, groups)
         def _(group):
@@ -317,12 +347,12 @@
         own = jnp.zeros((1, LANES), F32)
         cross = jnp.zeros((1, LANES), F32)
         for r in range(tile_rows):
-            cov = sea[r] * (cov_res[r] + scale[r] * back[r])
+            cov = sea[r] * (cov_res[r] + scale[r] * back[r, :layers])
             now = residual[r]
             img = cov + obs_error[r] * now
             cov_res[r] = cov
             image[r] = img
-            f_send[r] = scale[r] * (sea[r] * img)
+            f_send[r, :layers] = scale[r] * (sea[r] * img)
             own = own + jnp.sum(now * now, axis=0, keepdims=True)
             cross = cross + jnp.sum(now * img, axis=0, keepdims=True)
         p_send[iteration, 0:1] = own
@@ -347,20 +377,36 @@
         def _(rank):
             arrived(p_recv.at[iteration, rank], p_rsem.at[iteration, rank])
 
-        total = jnp.sum(jnp.sum(p_recv[iteration], axis=0), axis=1, keepdims=True)
-        norm_next, product = total[0:1], total[1:2]
+        sums = jnp.sum(jnp.sum(p_recv[iteration], axis=0), axis=1, keepdims=True)
+        norm_next, product = sums[0:1], sums[1:2]
         ratio = jnp.where(iteration == 0, 0.0, norm_next / norm)
         alpha = norm_next / (product - ratio * norm_next / alpha)
+        along_terms = [
+            ratio * term + jnp.where(iteration == n, 1.0, 0.0)
+            for n, term in enumerate(along_terms)
+        ]
+        weight_terms = [w + alpha * d for w, d in zip(weight_terms, along_terms)]
+        residual_sent()
         for r in range(tile_rows):
-            step_to = residual[r] + ratio * direction[r]
-            direction[r] = step_to
-            weights[r] = weights[r] + alpha * step_to
+            img = image[r] + ratio * along[r]
+            along[r] = img
+            now = residual[r] - alpha * img
+            residual[r] = now
+            r_send[r] = (sea[r] * now).astype(BF16)
+
+        @pl.when(iteration < ITERATIONS - 1)
+        def _():
+            send_residual(iteration + 1)
+
+        for r in range(tile_rows):
             cov = cov_res[r] + ratio * cov_dir[r]
             cov_dir[r] = cov
             increment[r] = increment[r] + alpha * cov
-            img = image[r] + ratio * along[r]
-            along[r] = img
-            residual[r] = residual[r] - alpha * img
+
+        @pl.loop(1, n_blocks)
+        def _(step):
+            origin = lax.rem(block - step + n_blocks, n_blocks)
+            sent(part_of(origin), s_ssem.at[origin], origin * n_gy + column)
 
         @pl.loop(0, n_dev)
         def _(rank):
@@ -372,42 +418,25 @@
             def _(rank):
                 sent(grid_slot(levels[0][1], rank), b_ssem.at[rank], rank)
 
-        return alpha, ratio, norm_next
+        return alpha, ratio, norm_next, along_terms, weight_terms
 
     one = jnp.ones((1, 1), F32)
-    lax.fori_loop(0, ITERATIONS, iterate, (-one, one * 0.0, one))
-
-    for r in range(tile_rows):
-        w_send[r] = (sea[r] * weights[r]).astype(BF16)
+    none = [one * 0.0] * ITERATIONS
+    state = lax.fori_loop(0, ITERATIONS, iterate, (-one, one * 0.0, one, none, none))
+    weight_terms = state[-1]
 
     @pl.loop(0, n_blocks)
-    def _(step):
-        target = lax.rem(block + step, n_blocks)
-        send(
-            w_send,
-            gathered.at[block],
-            w_ssem.at[target],
-            w_rsem.at[block],
-            target * n_gy + column,
-        )
-
-    @pl.loop(0, n_blocks)
-    def _(step):
-        origin = lax.rem(block - step + n_blocks, n_blocks)
-        arrived(gathered.at[origin], w_rsem.at[origin])
+    def _(origin):
         for r in range(tile_rows):
-            image[r] = gathered[origin, r].astype(F32)
-
-        @pl.loop(0, per_block)
+            image[r] = sum(
+                term * gathered[n, origin, r].astype(F32) for n, term in enumerate(weight_terms)
+            )
+
+        @pl.loop(0, count)
         def _(k):
-            mixed = mix(members[origin, k], image)
+            mixed = mix([members[k, origin * tile_rows + r] for r in range(tile_rows)], image)
             for r in range(tile_rows):
-                alpha_fields[k, origin, r] = mixed[r].astype(BF16)
-
-    @pl.loop(0, n_blocks)
-    def _(target):
-        sent(w_send, w_ssem.at[target], target * n_gy + column)
-        sent(members.at[target], m_ssem.at[target], target * n_gy + column)
+                alpha_fields[k, origin * tile_rows + r] = mixed[r].astype(BF16)
 
 
 def local(sizes, members, spread, sea_mask, innovations, obs_error, static_scale):
@@ -418,44 +447,41 @@
     tile_rows = innovations.shape[1]
     groups = -(-layers // SUB)
     padded = groups * SUB
-    extra = padded - layers
     grid_rows = rows
     width = lanes * n_gy
 
-    by_row = members.reshape(count, layers, n_blocks, tile_rows, lanes).transpose(2, 0, 3, 1, 4)
-    by_row = jnp.pad(by_row, ((0, 0), (0, 0), (0, 0), (0, extra), (0, 0)))
-
     def field(values):
-        return jnp.pad(values.transpose(1, 0, 2), ((0, 0), (0, extra), (0, 0)))
+        return values.transpose(1, 0, 2)
 
     sea = sea_mask.astype(F32)[:, None, :]
-    spread = jnp.pad(spread, ((0, extra), (0, extra)))
-    tile = (tile_rows, padded, lanes)
+    tile = (tile_rows, layers, lanes)
+    wide = (tile_rows, padded, lanes)
     f_tile = pltpu.VMEM(tile, F32)
     scratch = [
-        pltpu.VMEM((n_blocks, count, *tile), BF16),
+        pltpu.VMEM((ITERATIONS, n_blocks, *tile), BF16),
+        pltpu.VMEM(tile, BF16),
         pltpu.VMEM((n_blocks, *tile), BF16),
-        pltpu.VMEM(tile, BF16),
     ]
-    scratch += [f_tile] * 9
+    scratch += [f_tile] * 6
     scratch += [
+        pltpu.VMEM(wide, F32),
+        pltpu.VMEM(wide, F32),
         pltpu.VMEM((ITERATIONS, 2, lanes), F32),
         pltpu.VMEM((ITERATIONS, n_dev, 2, lanes), F32),
-        pltpu.VMEM((grid_rows + 2, SUB, width), F32),
         pltpu.VMEM((grid_rows + 2, SUB, width), F32),
     ]
     for level in range(GRIDS):
         scratch += [pltpu.VMEM((grid_rows // 2**level + 2, SUB, width), F32)] * 3
     dma = pltpu.SemaphoreType.DMA
     scratch += [
-        dma((n_blocks,)),
-        dma((n_blocks,)),
         dma((groups,)),
         dma((n_dev,)),
         dma((n_dev,)),
         dma((groups,)),
         dma((ITERATIONS, n_dev)),
         dma((ITERATIONS, n_dev)),
+        dma((n_blocks,)),
+        dma((ITERATIONS, n_blocks)),
         dma((n_blocks,)),
         dma((n_blocks,)),
     ]
@@ -464,19 +490,17 @@
         functools.partial(kernel, sizes, groups),
         out_shape=(
             jax.ShapeDtypeStruct(tile, F32),
-            jax.ShapeDtypeStruct((count, n_blocks, *tile), BF16),
+            jax.ShapeDtypeStruct((count, rows, layers, lanes), BF16),
         ),
         in_specs=[vmem] * 6,
         out_specs=(vmem, vmem),
         scratch_shapes=scratch,
         compiler_params=pltpu.CompilerParams(
-            collective_id=0, has_side_effects=True, vmem_limit_bytes=60 * 2**20
+            collective_id=0, has_side_effects=True, vmem_limit_bytes=64000 * 2**10
         ),
         name="window",
-    )(by_row, spread, sea, field(innovations), field(obs_error), field(static_scale))
-    increment = increment[:, :layers].transpose(1, 0, 2)
-    alpha_fields = alpha_fields.reshape(count, rows, padded, lanes)[:, :, :layers]
-    return increment, alpha_fields.transpose(0, 2, 1, 3)
+    )(members.transpose(0, 2, 1, 3), spread, sea, field(innovations), field(obs_error), field(static_scale))
+    return increment.transpose(1, 0, 2), alpha_fields.transpose(0, 2, 1, 3)
 
 
 def solution(mesh):

time: 235 us -> 178 us (0.76)
  Pallas kernels: 209 us -> 159 us
  local copies, waits for them, and re-layouts: 23.2 us -> 17.6 us
    pallas_call x1, Pallas kernels: 209 us -> 159 us  [local(): pl.pallas_call(functools.partial(kernel, sizes, groups), out_shape=(jax.S...]
    pad x5 -> x0, local copies, waits for them, and re-layouts: 7.17 us -> none  [the longest x1 3.77 us: local(): by_row = jnp.pad(by_row, ((0, 0), (0, 0), (0, 0), (0, extra), (0, 0)))]
    unnamed x5 -> x4, local copies, waits for them, and re-layouts: 9.5 us -> 15.9 us
    reshape x1 -> x0, local copies, waits for them, and re-layouts: 5.56 us -> none  [local(): members.reshape(count, layers, n_blocks, tile_rows, lanes)]
where the time goes in v2:
time: 178 us
  Pallas kernels  159 us (89%)
  local copies, waits for them, and re-layouts  17.6 us (10%)
    pallas_call x1, Pallas kernels, local(): pl.pallas_call(functools.partial(kernel, sizes, groups), out_shape=(jax.S...  159 us
    unnamed x4, local copies, waits for them, and re-layouts  15.9 us

profile of v2, /device:TPU:0, one launch (start us, length us, event | category | flops | bytes accessed | tf_op | source)
XLA Modules:
  0.0 178.1 jit_solution(17025097653554236357)
XLA Ops:
  0.6 1.3 convert_element_type.3
  1.9 1.6 copy.19
  3.5 1.8 copy_bitcast_fusion.1
  5.2 6.6 %copy.18 = bf16[8,75,32,128]{3,1,2,0:T(8,128)(2,1)} copy(bf16[8,75,32,128]{3,2,1,0:T(8,128)(2,1)} %param.6) | data formatting | bytes 9830400 | tf_op args[0]
  11.9 158.5 %window.1 = (f32[4,75,128]{2,1,0:T(8,128)}, bf16[8,32,75,128]{3,2,1,0:T(8,128)(2,1)}) custom-call(bf16[8,32,75,128]{3,2,1,0:T(8,128)(2,1)} %bitcast.13, bf16[75,75]{1,0:T(8,128)(2,1)} %spread.1, f32[4,1,128]{2,1,0:T(1,128)} %bitcast.17, f32[4,75,128]{2,1,0:T(8,128)} %bitcast.15, f32[4,75,128]{2,1,0:T(8,128)} %get-tuple-element.9.obs_error, ...), custom_call_target="tpu_custom_call" | custom-call | tf_op jit(solution)/shard_map/window/pallas_call | solution.py:489
  170.4 1.6 copy.12
  172.1 6.0 %copy.13 = bf16[8,75,32,128]{3,2,1,0:T(8,128)(2,1)} copy(bf16[8,75,32,128]{3,1,2,0:T(8,128)(2,1)} %bitcast.14) | data formatting | bytes 9830400

commit v3 on v2

--- a/solution.py
+++ b/solution.py
@@ -125,6 +125,8 @@
     gathered,
     r_send,
     s_recv,
+    e_recv,
+    own_sum,
     residual,
     along,
     cov_dir,
@@ -140,13 +142,15 @@
 ):
     n_ens, n_gx, n_gy = sizes
     level_refs = rest[: 3 * GRIDS]
-    (f_ssem, f_rsem, b_ssem, b_rsem, p_ssem, p_rsem, r_ssem, r_rsem, s_ssem, s_rsem) = rest[3 * GRIDS :]
+    (f_ssem, f_rsem, b_ssem, b_rsem, p_ssem, p_rsem, r_ssem, r_rsem, x_ssem, s_ssem, s_rsem, e_ssem, e_rsem) = rest[3 * GRIDS :]
     levels = [level_refs[3 * g : 3 * g + 3] for g in range(GRIDS)]
     f_res, f_recv = levels[0][0], levels[0][2]
     n_blocks = n_ens * n_gx
     n_dev = n_blocks * n_gy
     spacing = n_dev // groups
-    block = lax.axis_index("ens") * n_gx + lax.axis_index("gx")
+    my_ens = lax.axis_index("ens")
+    my_gx = lax.axis_index("gx")
+    block = my_ens * n_gx + my_gx
     column = lax.axis_index("gy")
     me = block * n_gy + column
     is_owner = (lax.rem(me, spacing) == 0) & (me // spacing < groups)
@@ -244,22 +248,27 @@
     def part_of(origin):
         return alpha_fields.at[0, pl.ds(origin * tile_rows, tile_rows)]
 
+    def peer(ens, gx):
+        return (ens * n_gx + gx) * n_gy + column
+
     def send_residual(iteration):
-        @pl.loop(0, n_blocks)
-        def _(step):
-            target = lax.rem(block + step, n_blocks)
+        def to(ens):
             send(
                 r_send,
                 gathered.at[iteration, block],
-                r_ssem.at[target],
+                r_ssem.at[ens],
                 r_rsem.at[iteration, block],
-                target * n_gy + column,
+                peer(ens, my_gx),
             )
 
+        @pl.loop(0, n_ens)
+        def _(step):
+            to(lax.rem(my_ens + step, n_ens))
+
     def residual_sent():
-        @pl.loop(0, n_blocks)
-        def _(target):
-            sent(r_send, r_ssem.at[target], target * n_gy + column)
+        @pl.loop(0, n_ens)
+        def _(ens):
+            sent(r_send, r_ssem.at[ens], peer(ens, my_gx))
 
     send_source()
     send_residual(0)
@@ -300,10 +309,26 @@
                     rank,
                 )
 
-        @pl.loop(0, n_blocks)
+        def tile_of(origin):
+            return gathered.at[iteration, origin]
+
+        @pl.loop(0, n_ens)
         def _(step):
-            origin = lax.rem(block - step + n_blocks, n_blocks)
-            arrived(gathered.at[iteration, origin], r_rsem.at[iteration, origin])
+            origin = lax.rem(my_ens - step + n_ens, n_ens) * n_gx + my_gx
+            arrived(tile_of(origin), r_rsem.at[iteration, origin])
+
+            @pl.loop(1, n_gx)
+            def _(hop):
+                gx = lax.rem(my_gx + hop, n_gx)
+                send(
+                    tile_of(origin),
+                    tile_of(origin),
+                    x_ssem.at[origin // n_gx, gx],
+                    r_rsem.at[iteration, origin],
+                    peer(my_ens, gx),
+                )
+
+        def partial_sum(origin):
             for r in range(tile_rows):
                 image[r] = gathered[iteration, origin, r].astype(F32)
                 total[r] = jnp.zeros_like(total[r])
@@ -315,29 +340,65 @@
                 for r in range(tile_rows):
                     total[r] = total[r] + values[r].astype(F32) * mixed[r]
 
-            @pl.when(step == 0)
-            def _():
-                for r in range(tile_rows):
-                    cov_res[r] = total[r]
-
-            @pl.when(step > 0)
-            def _():
+        @pl.loop(0, n_ens)
+        def _(ens):
+            partial_sum(ens * n_gx + my_gx)
+            for r in range(tile_rows):
+                own_sum[ens, r] = total[r]
+
+        @pl.loop(1, n_gx)
+        def _(hop):
+            gx = lax.rem(my_gx + hop, n_gx)
+
+            @pl.loop(1, n_ens + 1)
+            def _(step):
+                ens = lax.rem(my_ens - step + n_ens, n_ens)
+                origin = ens * n_gx + gx
+                arrived(tile_of(origin), r_rsem.at[iteration, origin])
+                partial_sum(origin)
                 for r in range(tile_rows):
                     alpha_fields[0, origin * tile_rows + r] = total[r].astype(BF16)
                 send(
                     part_of(origin),
-                    s_recv.at[block],
-                    s_ssem.at[origin],
-                    s_rsem.at[block],
-                    origin * n_gy + column,
+                    s_recv.at[my_gx, ens],
+                    s_ssem.at[ens, gx],
+                    s_rsem.at[my_gx, ens],
+                    peer(my_ens, gx),
                 )
 
-        @pl.loop(1, n_blocks)
+        @pl.loop(1, n_ens + 1)
         def _(step):
-            origin = lax.rem(block - step + n_blocks, n_blocks)
-            arrived(s_recv.at[origin], s_rsem.at[origin])
+            ens = lax.rem(my_ens - step + n_ens, n_ens)
+            origin = ens * n_gx + my_gx
+
+            @pl.loop(1, n_gx)
+            def _(hop):
+                gx = lax.rem(my_gx + hop, n_gx)
+                arrived(s_recv.at[gx, ens], s_rsem.at[gx, ens])
+                for r in range(tile_rows):
+                    own_sum[ens, r] = own_sum[ens, r] + s_recv[gx, ens, r].astype(F32)
+
+            @pl.when(step < n_ens)
+            def _():
+                for r in range(tile_rows):
+                    alpha_fields[0, origin * tile_rows + r] = own_sum[ens, r].astype(BF16)
+                send(
+                    part_of(origin),
+                    e_recv.at[my_ens],
+                    e_ssem.at[ens],
+                    e_rsem.at[my_ens],
+                    peer(ens, my_gx),
+                )
+
+        for r in range(tile_rows):
+            cov_res[r] = own_sum[my_ens, r]
+
+        @pl.loop(1, n_ens)
+        def _(step):
+            ens = lax.rem(my_ens - step + n_ens, n_ens)
+            arrived(e_recv.at[ens], e_rsem.at[ens])
             for r in range(tile_rows):
-                cov_res[r] = cov_res[r] + s_recv[origin, r].astype(F32)
+                cov_res[r] = cov_res[r] + e_recv[ens, r].astype(F32)
 
         @pl.loop(0, groups)
         def _(group):
@@ -403,10 +464,15 @@
             cov_dir[r] = cov
             increment[r] = increment[r] + alpha * cov
 
-        @pl.loop(1, n_blocks)
-        def _(step):
-            origin = lax.rem(block - step + n_blocks, n_blocks)
-            sent(part_of(origin), s_ssem.at[origin], origin * n_gy + column)
+        @pl.loop(0, n_ens)
+        def _(ens):
+            @pl.loop(1, n_gx)
+            def _(hop):
+                gx = lax.rem(my_gx + hop, n_gx)
+                sent(part_of(block), s_ssem.at[ens, gx], peer(my_ens, gx))
+                sent(tile_of(block), x_ssem.at[ens, gx], peer(my_ens, gx))
+
+            sent(part_of(block), e_ssem.at[ens], peer(ens, my_gx))
 
         @pl.loop(0, n_dev)
         def _(rank):
@@ -460,7 +526,9 @@
     scratch = [
         pltpu.VMEM((ITERATIONS, n_blocks, *tile), BF16),
         pltpu.VMEM(tile, BF16),
-        pltpu.VMEM((n_blocks, *tile), BF16),
+        pltpu.VMEM((n_gx, n_ens, *tile), BF16),
+        pltpu.VMEM((n_ens, *tile), BF16),
+        pltpu.VMEM((n_ens, *tile), F32),
     ]
     scratch += [f_tile] * 6
     scratch += [
@@ -480,10 +548,13 @@
         dma((groups,)),
         dma((ITERATIONS, n_dev)),
         dma((ITERATIONS, n_dev)),
-        dma((n_blocks,)),
+        dma((n_ens,)),
         dma((ITERATIONS, n_blocks)),
-        dma((n_blocks,)),
-        dma((n_blocks,)),
+        dma((n_ens, n_gx)),
+        dma((n_ens, n_gx)),
+        dma((n_gx, n_ens)),
+        dma((n_ens,)),
+        dma((n_ens,)),
     ]
     vmem = pl.BlockSpec(memory_space=pltpu.VMEM)
     increment, alpha_fields = pl.pallas_call(

time: 178 us -> 154 us (0.87)
  Pallas kernels: 159 us -> 134 us
    pallas_call x1, Pallas kernels: 159 us -> 134 us  [local(): pl.pallas_call(functools.partial(kernel, sizes, groups), out_shape=(jax.S...]
where the time goes in v3:
time: 154 us; the launch traced here: 153 us
  Pallas kernels  134 us (87%)
  local copies, waits for them, and re-layouts  17.6 us (11%)
    pallas_call x1, Pallas kernels, local(): pl.pallas_call(functools.partial(kernel, sizes, groups), out_shape=(jax.S...  134 us
    unnamed x4, local copies, waits for them, and re-layouts  15.9 us

profile of v3, /device:TPU:0, one launch (start us, length us, event | category | flops | bytes accessed | tf_op | source)
XLA Modules:
  0.0 153.4 jit_solution(1529843441496909306)
XLA Ops:
  0.6 1.3 convert_element_type.3
  1.9 1.6 %copy.19 = f32[75,4,128]{2,0,1:T(8,128)} copy(f32[75,4,128]{2,1,0:T(4,128)} %param.9) | data formatting | bytes 307200 | tf_op args[3]
  3.5 1.8 %copy_bitcast_fusion.1 = (f32[4,75,128]{2,1,0:T(8,128)}, f32[4,75,128]{2,1,0:T(8,128)}) fusion(f32[75,4,128]{2,1,0:T(4,128)} %param.11, f32[75,4,128]{2,1,0:T(4,128)} %param.10), kind=kLoop, calls=%fused_computation.1 | loop fusion | bytes 614400 | tf_op jit(solution)/shard_map/transpose | solution.py:520
  5.2 6.6 %copy.18 = bf16[8,75,32,128]{3,1,2,0:T(8,128)(2,1)} copy(bf16[8,75,32,128]{3,2,1,0:T(8,128)(2,1)} %param.6) | data formatting | bytes 9830400 | tf_op args[0]
  11.9 133.8 %window.1 = (f32[4,75,128]{2,1,0:T(8,128)}, bf16[8,32,75,128]{3,2,1,0:T(8,128)(2,1)}) custom-call(bf16[8,32,75,128]{3,2,1,0:T(8,128)(2,1)} %bitcast.13, bf16[75,75]{1,0:T(8,128)(2,1)} %spread.1, f32[4,1,128]{2,1,0:T(1,128)} %bitcast.17, f32[4,75,128]{2,1,0:T(8,128)} %bitcast.15, f32[4,75,128]{2,1,0:T(8,128)} %get-tuple-element.9.obs_error, ...), custom_call_target="tpu_custom_call" | custom-call | tf_op jit(solution)/shard_map/window/pallas_call | solution.py:560
  145.7 1.6 %copy.12 = f32[75,4,128]{2,1,0:T(4,128)} copy(f32[75,4,128]{2,0,1:T(8,128)} %bitcast.16) | data formatting | bytes 307200
  147.3 6.0 %copy.13 = bf16[8,75,32,128]{3,2,1,0:T(8,128)(2,1)} copy(bf16[8,75,32,128]{3,1,2,0:T(8,128)(2,1)} %bitcast.14) | data formatting | bytes 9830400
